TPU v7x, 32 devices: a whole 2x2x4 slice. The times are simulated.
32 devices in a mesh: groups: 2 (over y), ctx: 4 (over z), head: 2 (over x), rep: 2 (over core).
Axes of the slice: x: 2, y: 2, z: 4, core: 2. Of those that a mesh axis runs over, the one named last changes fastest.
Arguments:
- queries: bfloat16 [12288, 1536], P(('groups', 'ctx', 'rep'), 'head'), parts along dimension 0, may hold values from -5 to 5
- keys_in: bfloat16 [12288, 1536], P(('groups', 'ctx', 'rep'), 'head'), parts along dimension 0, may hold values from -12 to 12
- values: bfloat16 [12288, 1536], P(('groups', 'ctx', 'rep'), 'head'), parts along dimension 0, may hold values from -6 to 6
- grad_out: bfloat16 [12288, 1536], P(('groups', 'ctx', 'rep'), 'head'), parts along dimension 0, may hold values from -6 to 6
- clip_ids: int32 [16], P('groups'), parts along dimension 0, may hold values from 0 to 2, as said below
Outputs:
- grad_query: bfloat16 [12288, 1536], P(('groups', 'ctx', 'rep'), 'head'), parts along dimension 0
- grad_key: bfloat16 [12288, 1536], P(('groups', 'ctx', 'rep'), 'head'), parts along dimension 0
- grad_value: bfloat16 [12288, 1536], P(('groups', 'ctx', 'rep'), 'head'), parts along dimension 0
There are 2 independent parts, one for each index of `groups`. A program takes and returns all parts, laid end to end along the dimension named above; each array names one. Nothing has to cross between parts.
Inputs may be any that keep to these rules, and one draw needn't show every extreme that they name: clip_ids of the first tile row is 0, and each next tile row's id equals the previous one or exceeds it by one; a clip is the run of tile rows with one id; the last tile row's id is 2.
All inputs are finite; a program needn't handle non-finite values.
Results may differ from a plain program's by a relative error of at most 0.013.
Values may be sent and summed in bfloat16 or wider, within the bound.
A program may use at most 64 MiB of HBM per device.

v0:
```python
import jax
import jax.numpy as jnp
from jax import lax
from jax.sharding import PartitionSpec as P

HEAD_DIM = 128


def padded(value, sides, width):
    for axis, dim in sides:
        size, length = (lax.axis_size(axis), value.shape[dim])
        up = [(i, (i + 1) % size) for i in range(size - 1)]
        down = [(j, i) for i, j in up]
        last = lax.slice_in_dim(value, length - width, length, axis=dim)
        first = lax.slice_in_dim(value, 0, width, axis=dim)
        before = lax.ppermute(last, axis, up)
        after = lax.ppermute(first, axis, down)
        value = jnp.concatenate([before, value, after], axis=dim)
    return value


def from_behind(value, axis, by):
    length = lax.axis_size(axis)
    pairs = [(i, i + by) for i in range(length) if 0 <= i + by < length]
    return lax.ppermute(value, axis, pairs)


def nt_product(left, right):
    return lax.dot_general(
        left, right, (((1,), (1,)), ((), ())), preferred_element_type=jnp.float32
    )


def tn_product(left, right):
    return lax.dot_general(
        left, right, (((0,), (0,)), ((), ())), preferred_element_type=jnp.float32
    )


def nn_product(left, right):
    return jnp.dot(left, right, preferred_element_type=jnp.float32)


def per_device(queries, keys_in, values, grad_out, clip_ids):
    row_tok, feature_width = queries.shape
    head_count = feature_width // HEAD_DIM
    softmax_scale = HEAD_DIM ** (-0.5)
    position = lax.axis_index(("ctx", "rep"))
    row_count = lax.axis_size(("ctx", "rep"))
    own_clip = lax.dynamic_index_in_dim(clip_ids, position, 0, keepdims=False)
    below_clip = lax.dynamic_index_in_dim(clip_ids, jnp.maximum(position - 1, 0), 0, keepdims=False)
    above_clip = lax.dynamic_index_in_dim(
        clip_ids, jnp.minimum(position + 1, row_count - 1), 0, keepdims=False
    )
    block_valid = jnp.stack(
        [
            (position > 0) & (below_clip == own_clip),
            position >= 0,
            (position < row_count - 1) & (above_clip == own_clip),
        ]
    )
    key_mask = jnp.repeat(block_valid, row_tok)
    kv_pair = jnp.stack([keys_in, values])
    neighbour_kv = padded(kv_pair, ((("ctx", "rep"), 1),), row_tok)

    def one_head(head_index, partial_value):
        grad_q_all, key_all, value_all = partial_value
        head_start = head_index * HEAD_DIM
        q_head = lax.dynamic_slice_in_dim(queries, head_start, HEAD_DIM, 1)
        g_head = lax.dynamic_slice_in_dim(grad_out, head_start, HEAD_DIM, 1)
        k_head = lax.dynamic_slice_in_dim(neighbour_kv[0], head_start, HEAD_DIM, 1)
        v_head = lax.dynamic_slice_in_dim(neighbour_kv[1], head_start, HEAD_DIM, 1)
        scores = nt_product(q_head, k_head)
        dprob = nt_product(g_head, v_head)
        scores = jnp.where(key_mask[None, :], scores * softmax_scale, -jnp.inf)
        row_max = jnp.max(scores, axis=1, keepdims=True)
        log_total = row_max + jnp.log(jnp.sum(jnp.exp(scores - row_max), axis=1, keepdims=True))
        probs = jnp.exp(scores - log_total)
        probs_low = probs.astype(jnp.bfloat16)
        row_delta = jnp.sum(probs * dprob, axis=1, keepdims=True)
        dscores = (probs * (dprob - row_delta)).astype(jnp.bfloat16)
        grad_q_head = nn_product(dscores, k_head)
        key_terms = tn_product(dscores, q_head)
        value_terms = tn_product(probs_low, g_head)
        grad_q_all = lax.dynamic_update_slice_in_dim(
            grad_q_all, (grad_q_head * softmax_scale).astype(jnp.bfloat16), head_start, 1
        )
        key_all = lax.dynamic_update_slice_in_dim(
            key_all, (key_terms * softmax_scale).astype(jnp.bfloat16), head_start, 1
        )
        value_all = lax.dynamic_update_slice_in_dim(
            value_all, value_terms.astype(jnp.bfloat16), head_start, 1
        )
        return (grad_q_all, key_all, value_all)

    initial = (
        jnp.zeros((row_tok, feature_width), jnp.bfloat16),
        jnp.zeros((3 * row_tok, feature_width), jnp.bfloat16),
        jnp.zeros((3 * row_tok, feature_width), jnp.bfloat16),
    )
    grad_query, key_all, value_all = lax.fori_loop(0, head_count, one_head, initial)
    lower_terms = jnp.stack([key_all[:row_tok], value_all[:row_tok]])
    upper_terms = jnp.stack([key_all[2 * row_tok :], value_all[2 * row_tok :]])
    from_above = from_behind(lower_terms, ("ctx", "rep"), -1)
    from_below = from_behind(upper_terms, ("ctx", "rep"), 1)
    middle_keys = key_all[row_tok : 2 * row_tok].astype(jnp.float32)
    middle_values = value_all[row_tok : 2 * row_tok].astype(jnp.float32)
    grad_key = (
        middle_keys + from_above[0].astype(jnp.float32) + from_below[0].astype(jnp.float32)
    ).astype(jnp.bfloat16)
    grad_value = (
        middle_values + from_above[1].astype(jnp.float32) + from_below[1].astype(jnp.float32)
    ).astype(jnp.bfloat16)
    return (grad_query, grad_key, grad_value)


def solution(mesh):
    in_specs = (
        P(("groups", "ctx", "rep"), "head"),
        P(("groups", "ctx", "rep"), "head"),
        P(("groups", "ctx", "rep"), "head"),
        P(("groups", "ctx", "rep"), "head"),
        P("groups"),
    )
    out_specs = (
        P(("groups", "ctx", "rep"), "head"),
        P(("groups", "ctx", "rep"), "head"),
        P(("groups", "ctx", "rep"), "head"),
    )
    return jax.shard_map(
        per_device, mesh=mesh, in_specs=in_specs, out_specs=out_specs, check_vma=False
    )
```

profile of v0, /device:TPU:1, one launch (start us, length us, event | category | flops | bytes accessed | tf_op | source)
XLA Modules:
  0.0 207.4 jit_solution(14953918204046823691)
XLA Ops:
  0.7 3.4 %pad_maximum_fusion.1 = bf16[2,768,768]{2,1,0:T(8,128)(2,1)} fusion(bf16[1,768,768]{2,1,0:T(8,128)(2,1)} %bitcast.59, bf16[1,768,768]{2,1,0:T(8,128)(2,1)} %bitcast.61), kind=kLoop, calls=%fused_computation.34 | loop fusion | flops 1179648 | bytes 4718592 | tf_op jit(solution)/shard_map/stack | solution.py:63
  4.1 2.0 collective-permute-start.1
  6.0 4.6 %collective-permute-start = (bf16[2,768,768]{2,1,0:T(8,128)(2,1)}, bf16[2,768,768]{2,1,0:T(8,128)(2,1)}, u32[]{:S(2)}, u32[]{:S(2)}) collective-permute-start(bf16[2,768,768]{2,1,0:T(8,128)(2,1)} %pad_maximum_fusion.1), channel_id=1, source_target_pairs={{0,1},{1,4},{4,5},{5,8},{8,9},{9,12},{12,13},{2,3},{3,6},{6,7},{7,... | collective-permute-start | bytes 7077896 | tf_op jit(solution)/shard_map/ppermute | solution.py:16
  13.9 21.6 %collective-permute-done.1 = bf16[2,768,768]{2,1,0:T(8,128)(2,1)} collective-permute-done((bf16[2,768,768]{2,1,0:T(8,128)(2,1)}, bf16[2,768,768]{2,1,0:T(8,128)(2,1)}, u32[]{:S(2)}, u32[]{:S(2)}) %collective-permute-start.1) | collective-permute-done | bytes 2359328 | tf_op jit(solution)/shard_map/ppermute | solution.py:17
  36.7 12.4 %pad_maximum_fusion = bf16[2,2304,768]{2,1,0:T(8,128)(2,1)} fusion(bf16[2,768,768]{2,1,0:T(8,128)(2,1)} %collective-permute-done.1, bf16[1,768,768]{2,1,0:T(8,128)(2,1)S(1)} %bitcast.60, bf16[1,768,768]{2,1,0:T(8,128)(2,1)S(1)} %bitcast.62, bf16[2,768,768]{2,1,0:T(8,128)(2,1)} %collective-permute-done), kind=kLoop, calls=%fused_computation.33 | loop fusion | flops 28311552 | bytes 14155776 | tf_op jit(solution)/shard_map/concatenate | solution.py:18
  50.4 2.1 broadcast.26
  52.4 114.4 %while.18 = (s32[]{:T(128)}, bf16[768,768]{1,0:T(8,128)(2,1)}, bf16[2304,768]{1,0:T(8,128)(2,1)}, bf16[2304,768]{1,0:T(8,128)(2,1)S(1)}, bf16[768,768]{1,0:T(8,1...) while((s32[]{:T(128)}, bf16[768,768]{1,0:T(8,128)(2,1)}, ...), condition=%wide.region_4.5_spmd.clone, body=%wide.region_0.4_spmd.clone.sunk | while | flops 2290776576 | bytes 78301096 | solution.py:101
  52.5 3.5 %fusion.50 = (bf16[1,2304,768]{2,1,0:T(8,128)(2,1)S(1)}, bf16[1,2304,768]{2,1,0:T(8,128)(2,1)S(1)}) fusion(bf16[2,2304,768]{2,1,0:T(8,128)(2,1)} %get-tuple-element.289), kind=kLoop, calls=%fused_computation.52.clone.1 | loop fusion | bytes 14155776 | tf_op jit(solution)/shard_map/while/body/eval_jaxpr/slice | solution.py:71
  56.1 2.2 %fusion.51 = (f32[768]{0:T(1024)S(1)}, f32[768,2304]{1,0:T(8,128)S(1)}) fusion(bf16[1,2304,768]{2,1,0:T(8,128)(2,1)S(1)} %get-tuple-element.254, s32[]{:T(128)S(6)} %select_n.35, bf16[768,768]{1,0:T(8,128)(2,1)} %get-tuple-element.288, pred[2304]{0:T(1024)(128)(4,1)S(1)} %broadcast_in_dim.57), kind=kOutput, calls=%fused_computation.53.clone.1 | convolution fusion | flops 458292480 | bytes 7871488 | tf_op jit(solution)/shard_map/while/body/eval_jaxpr/dot_general | solution.py:29
  59.4 2.7 %fusion.54 = bf16[2304,768]{1,0:T(8,128)(2,1)S(1)} fusion(bf16[2304,768]{1,0:T(8,128)(2,1)S(1)} %get-tuple-element.275, s32[]{:T(128)S(6)} %select_n.35, f32[768,2304]{1,0:T(8,128)S(1)} %get-tuple-element.255, f32[768]{0:T(1024)S(1)} %log_add_fusion.2, bf16[768,768]{1,0:T(8,128)(2,1)} %get-tuple-element.290), kind=kOutput, calls=%fused_computation.9.clone.1 | convolution fusion | flops 456818688 | bytes 7869440 | tf_op jit(solution)/shard_map/while/body/eval_jaxpr/dot_general | solution.py:35
  62.1 2.7 %multiply_reduce_fusion.2 = (f32[768]{0:T(1024)S(1)}, f32[768,2304]{1,0:T(8,128)S(1)}) fusion(f32[768,2304]{1,0:T(8,128)S(1)} %get-tuple-element.255, f32[768]{0:T(1024)S(1)} %log_add_fusion.2, bf16[1,2304,768]{2,1,0:T(8,128)(2,1)S(1)} %get-tuple-element.257, s32[]{:T(128)S(6)} %select_n.35, bf16[768,768]{1,0:T(8,128)(2,1)} %get-tuple-element.290), kind=kOutput, calls=%fused_computation.2.clone.1 | convolution fusion | flops 458292480 | bytes 14950400 | tf_op jit(solution)/shard_map/while/body/eval_jaxpr/dot_general | solution.py:29
  64.7 2.0 multiply_convert_fusion.2
  68.5 3.1 %fusion.53 = bf16[2304,768]{1,0:T(8,128)(2,1)} fusion(bf16[2304,768]{1,0:T(8,128)(2,1)} %get-tuple-element.274, s32[]{:T(128)S(6)} %select_n.35, bf16[768,2304]{1,0:T(8,128)(2,1)S(1)} %multiply_convert_fusion.2, bf16[768,768]{1,0:T(8,128)(2,1)} %get-tuple-element.288), kind=kOutput, calls=%fused_computation.11.clone.1 | convolution fusion | flops 453574656 | bytes 4326400 | tf_op jit(solution)/shard_map/while/body/eval_jaxpr/dot_general | solution.py:35
  71.7 3.5 %fusion.50 = (bf16[1,2304,768]{2,1,0:T(8,128)(2,1)S(1)}, bf16[1,2304,768]{2,1,0:T(8,128)(2,1)S(1)}) fusion(bf16[2,2304,768]{2,1,0:T(8,128)(2,1)} %get-tuple-element.289), kind=kLoop, calls=%fused_computation.52.clone.1 | loop fusion | bytes 14155776 | tf_op jit(solution)/shard_map/while/body/eval_jaxpr/slice | solution.py:71
  75.2 2.2 %fusion.51 = (f32[768]{0:T(1024)S(1)}, f32[768,2304]{1,0:T(8,128)S(1)}) fusion(bf16[1,2304,768]{2,1,0:T(8,128)(2,1)S(1)} %get-tuple-element.254, s32[]{:T(128)S(6)} %select_n.35, bf16[768,768]{1,0:T(8,128)(2,1)} %get-tuple-element.288, pred[2304]{0:T(1024)(128)(4,1)S(1)} %broadcast_in_dim.57), kind=kOutput, calls=%fused_computation.53.clone.1 | convolution fusion | flops 458292480 | bytes 7871488 | tf_op jit(solution)/shard_map/while/body/eval_jaxpr/dot_general | solution.py:29
  78.5 2.7 %fusion.54 = bf16[2304,768]{1,0:T(8,128)(2,1)S(1)} fusion(bf16[2304,768]{1,0:T(8,128)(2,1)S(1)} %get-tuple-element.275, s32[]{:T(128)S(6)} %select_n.35, f32[768,2304]{1,0:T(8,128)S(1)} %get-tuple-element.255, f32[768]{0:T(1024)S(1)} %log_add_fusion.2, bf16[768,768]{1,0:T(8,128)(2,1)} %get-tuple-element.290), kind=kOutput, calls=%fused_computation.9.clone.1 | convolution fusion | flops 456818688 | bytes 7869440 | tf_op jit(solution)/shard_map/while/body/eval_jaxpr/dot_general | solution.py:35
  81.2 2.7 %multiply_reduce_fusion.2 = (f32[768]{0:T(1024)S(1)}, f32[768,2304]{1,0:T(8,128)S(1)}) fusion(f32[768,2304]{1,0:T(8,128)S(1)} %get-tuple-element.255, f32[768]{0:T(1024)S(1)} %log_add_fusion.2, bf16[1,2304,768]{2,1,0:T(8,128)(2,1)S(1)} %get-tuple-element.257, s32[]{:T(128)S(6)} %select_n.35, bf16[768,768]{1,0:T(8,128)(2,1)} %get-tuple-element.290), kind=kOutput, calls=%fused_computation.2.clone.1 | convolution fusion | flops 458292480 | bytes 14950400 | tf_op jit(solution)/shard_map/while/body/eval_jaxpr/dot_general | solution.py:29
  83.9 2.0 multiply_convert_fusion.2
  87.6 3.0 %fusion.53 = bf16[2304,768]{1,0:T(8,128)(2,1)} fusion(bf16[2304,768]{1,0:T(8,128)(2,1)} %get-tuple-element.274, s32[]{:T(128)S(6)} %select_n.35, bf16[768,2304]{1,0:T(8,128)(2,1)S(1)} %multiply_convert_fusion.2, bf16[768,768]{1,0:T(8,128)(2,1)} %get-tuple-element.288), kind=kOutput, calls=%fused_computation.11.clone.1 | convolution fusion | flops 453574656 | bytes 4326400 | tf_op jit(solution)/shard_map/while/body/eval_jaxpr/dot_general | solution.py:35
  90.7 3.5 %fusion.50 = (bf16[1,2304,768]{2,1,0:T(8,128)(2,1)S(1)}, bf16[1,2304,768]{2,1,0:T(8,128)(2,1)S(1)}) fusion(bf16[2,2304,768]{2,1,0:T(8,128)(2,1)} %get-tuple-element.289), kind=kLoop, calls=%fused_computation.52.clone.1 | loop fusion | bytes 14155776 | tf_op jit(solution)/shard_map/while/body/eval_jaxpr/slice | solution.py:71
  94.2 2.2 %fusion.51 = (f32[768]{0:T(1024)S(1)}, f32[768,2304]{1,0:T(8,128)S(1)}) fusion(bf16[1,2304,768]{2,1,0:T(8,128)(2,1)S(1)} %get-tuple-element.254, s32[]{:T(128)S(6)} %select_n.35, bf16[768,768]{1,0:T(8,128)(2,1)} %get-tuple-element.288, pred[2304]{0:T(1024)(128)(4,1)S(1)} %broadcast_in_dim.57), kind=kOutput, calls=%fused_computation.53.clone.1 | convolution fusion | flops 458292480 | bytes 7871488 | tf_op jit(solution)/shard_map/while/body/eval_jaxpr/dot_general | solution.py:29
  97.5 2.7 %fusion.54 = bf16[2304,768]{1,0:T(8,128)(2,1)S(1)} fusion(bf16[2304,768]{1,0:T(8,128)(2,1)S(1)} %get-tuple-element.275, s32[]{:T(128)S(6)} %select_n.35, f32[768,2304]{1,0:T(8,128)S(1)} %get-tuple-element.255, f32[768]{0:T(1024)S(1)} %log_add_fusion.2, bf16[768,768]{1,0:T(8,128)(2,1)} %get-tuple-element.290), kind=kOutput, calls=%fused_computation.9.clone.1 | convolution fusion | flops 456818688 | bytes 7869440 | tf_op jit(solution)/shard_map/while/body/eval_jaxpr/dot_general | solution.py:35
  100.2 2.7 %multiply_reduce_fusion.2 = (f32[768]{0:T(1024)S(1)}, f32[768,2304]{1,0:T(8,128)S(1)}) fusion(f32[768,2304]{1,0:T(8,128)S(1)} %get-tuple-element.255, f32[768]{0:T(1024)S(1)} %log_add_fusion.2, bf16[1,2304,768]{2,1,0:T(8,128)(2,1)S(1)} %get-tuple-element.257, s32[]{:T(128)S(6)} %select_n.35, bf16[768,768]{1,0:T(8,128)(2,1)} %get-tuple-element.290), kind=kOutput, calls=%fused_computation.2.clone.1 | convolution fusion | flops 458292480 | bytes 14950400 | tf_op jit(solution)/shard_map/while/body/eval_jaxpr/dot_general | solution.py:29
  102.9 2.0 multiply_convert_fusion.2
  106.7 3.0 %fusion.53 = bf16[2304,768]{1,0:T(8,128)(2,1)} fusion(bf16[2304,768]{1,0:T(8,128)(2,1)} %get-tuple-element.274, s32[]{:T(128)S(6)} %select_n.35, bf16[768,2304]{1,0:T(8,128)(2,1)S(1)} %multiply_convert_fusion.2, bf16[768,768]{1,0:T(8,128)(2,1)} %get-tuple-element.288), kind=kOutput, calls=%fused_computation.11.clone.1 | convolution fusion | flops 453574656 | bytes 4326400 | tf_op jit(solution)/shard_map/while/body/eval_jaxpr/dot_general | solution.py:35
  109.7 3.5 %fusion.50 = (bf16[1,2304,768]{2,1,0:T(8,128)(2,1)S(1)}, bf16[1,2304,768]{2,1,0:T(8,128)(2,1)S(1)}) fusion(bf16[2,2304,768]{2,1,0:T(8,128)(2,1)} %get-tuple-element.289), kind=kLoop, calls=%fused_computation.52.clone.1 | loop fusion | bytes 14155776 | tf_op jit(solution)/shard_map/while/body/eval_jaxpr/slice | solution.py:71
  113.3 2.2 %fusion.51 = (f32[768]{0:T(1024)S(1)}, f32[768,2304]{1,0:T(8,128)S(1)}) fusion(bf16[1,2304,768]{2,1,0:T(8,128)(2,1)S(1)} %get-tuple-element.254, s32[]{:T(128)S(6)} %select_n.35, bf16[768,768]{1,0:T(8,128)(2,1)} %get-tuple-element.288, pred[2304]{0:T(1024)(128)(4,1)S(1)} %broadcast_in_dim.57), kind=kOutput, calls=%fused_computation.53.clone.1 | convolution fusion | flops 458292480 | bytes 7871488 | tf_op jit(solution)/shard_map/while/body/eval_jaxpr/dot_general | solution.py:29
  116.6 2.7 %fusion.54 = bf16[2304,768]{1,0:T(8,128)(2,1)S(1)} fusion(bf16[2304,768]{1,0:T(8,128)(2,1)S(1)} %get-tuple-element.275, s32[]{:T(128)S(6)} %select_n.35, f32[768,2304]{1,0:T(8,128)S(1)} %get-tuple-element.255, f32[768]{0:T(1024)S(1)} %log_add_fusion.2, bf16[768,768]{1,0:T(8,128)(2,1)} %get-tuple-element.290), kind=kOutput, calls=%fused_computation.9.clone.1 | convolution fusion | flops 456818688 | bytes 7869440 | tf_op jit(solution)/shard_map/while/body/eval_jaxpr/dot_general | solution.py:35
  119.3 2.7 %multiply_reduce_fusion.2 = (f32[768]{0:T(1024)S(1)}, f32[768,2304]{1,0:T(8,128)S(1)}) fusion(f32[768,2304]{1,0:T(8,128)S(1)} %get-tuple-element.255, f32[768]{0:T(1024)S(1)} %log_add_fusion.2, bf16[1,2304,768]{2,1,0:T(8,128)(2,1)S(1)} %get-tuple-element.257, s32[]{:T(128)S(6)} %select_n.35, bf16[768,768]{1,0:T(8,128)(2,1)} %get-tuple-element.290), kind=kOutput, calls=%fused_computation.2.clone.1 | convolution fusion | flops 458292480 | bytes 14950400 | tf_op jit(solution)/shard_map/while/body/eval_jaxpr/dot_general | solution.py:29
  121.9 2.0 multiply_convert_fusion.2
  125.7 3.0 %fusion.53 = bf16[2304,768]{1,0:T(8,128)(2,1)} fusion(bf16[2304,768]{1,0:T(8,128)(2,1)} %get-tuple-element.274, s32[]{:T(128)S(6)} %select_n.35, bf16[768,2304]{1,0:T(8,128)(2,1)S(1)} %multiply_convert_fusion.2, bf16[768,768]{1,0:T(8,128)(2,1)} %get-tuple-element.288), kind=kOutput, calls=%fused_computation.11.clone.1 | convolution fusion | flops 453574656 | bytes 4326400 | tf_op jit(solution)/shard_map/while/body/eval_jaxpr/dot_general | solution.py:35
  128.8 3.5 %fusion.50 = (bf16[1,2304,768]{2,1,0:T(8,128)(2,1)S(1)}, bf16[1,2304,768]{2,1,0:T(8,128)(2,1)S(1)}) fusion(bf16[2,2304,768]{2,1,0:T(8,128)(2,1)} %get-tuple-element.289), kind=kLoop, calls=%fused_computation.52.clone.1 | loop fusion | bytes 14155776 | tf_op jit(solution)/shard_map/while/body/eval_jaxpr/slice | solution.py:71
  132.4 2.2 %fusion.51 = (f32[768]{0:T(1024)S(1)}, f32[768,2304]{1,0:T(8,128)S(1)}) fusion(bf16[1,2304,768]{2,1,0:T(8,128)(2,1)S(1)} %get-tuple-element.254, s32[]{:T(128)S(6)} %select_n.35, bf16[768,768]{1,0:T(8,128)(2,1)} %get-tuple-element.288, pred[2304]{0:T(1024)(128)(4,1)S(1)} %broadcast_in_dim.57), kind=kOutput, calls=%fused_computation.53.clone.1 | convolution fusion | flops 458292480 | bytes 7871488 | tf_op jit(solution)/shard_map/while/body/eval_jaxpr/dot_general | solution.py:29
  135.6 2.7 %fusion.54 = bf16[2304,768]{1,0:T(8,128)(2,1)S(1)} fusion(bf16[2304,768]{1,0:T(8,128)(2,1)S(1)} %get-tuple-element.275, s32[]{:T(128)S(6)} %select_n.35, f32[768,2304]{1,0:T(8,128)S(1)} %get-tuple-element.255, f32[768]{0:T(1024)S(1)} %log_add_fusion.2, bf16[768,768]{1,0:T(8,128)(2,1)} %get-tuple-element.290), kind=kOutput, calls=%fused_computation.9.clone.1 | convolution fusion | flops 456818688 | bytes 7869440 | tf_op jit(solution)/shard_map/while/body/eval_jaxpr/dot_general | solution.py:35
  138.4 2.7 %multiply_reduce_fusion.2 = (f32[768]{0:T(1024)S(1)}, f32[768,2304]{1,0:T(8,128)S(1)}) fusion(f32[768,2304]{1,0:T(8,128)S(1)} %get-tuple-element.255, f32[768]{0:T(1024)S(1)} %log_add_fusion.2, bf16[1,2304,768]{2,1,0:T(8,128)(2,1)S(1)} %get-tuple-element.257, s32[]{:T(128)S(6)} %select_n.35, bf16[768,768]{1,0:T(8,128)(2,1)} %get-tuple-element.290), kind=kOutput, calls=%fused_computation.2.clone.1 | convolution fusion | flops 458292480 | bytes 14950400 | tf_op jit(solution)/shard_map/while/body/eval_jaxpr/dot_general | solution.py:29
  141.0 2.0 multiply_convert_fusion.2
  144.8 3.0 %fusion.53 = bf16[2304,768]{1,0:T(8,128)(2,1)} fusion(bf16[2304,768]{1,0:T(8,128)(2,1)} %get-tuple-element.274, s32[]{:T(128)S(6)} %select_n.35, bf16[768,2304]{1,0:T(8,128)(2,1)S(1)} %multiply_convert_fusion.2, bf16[768,768]{1,0:T(8,128)(2,1)} %get-tuple-element.288), kind=kOutput, calls=%fused_computation.11.clone.1 | convolution fusion | flops 453574656 | bytes 4326400 | tf_op jit(solution)/shard_map/while/body/eval_jaxpr/dot_general | solution.py:35
  147.9 3.5 %fusion.50 = (bf16[1,2304,768]{2,1,0:T(8,128)(2,1)S(1)}, bf16[1,2304,768]{2,1,0:T(8,128)(2,1)S(1)}) fusion(bf16[2,2304,768]{2,1,0:T(8,128)(2,1)} %get-tuple-element.289), kind=kLoop, calls=%fused_computation.52.clone.1 | loop fusion | bytes 14155776 | tf_op jit(solution)/shard_map/while/body/eval_jaxpr/slice | solution.py:71
  151.4 2.2 %fusion.51 = (f32[768]{0:T(1024)S(1)}, f32[768,2304]{1,0:T(8,128)S(1)}) fusion(bf16[1,2304,768]{2,1,0:T(8,128)(2,1)S(1)} %get-tuple-element.254, s32[]{:T(128)S(6)} %select_n.35, bf16[768,768]{1,0:T(8,128)(2,1)} %get-tuple-element.288, pred[2304]{0:T(1024)(128)(4,1)S(1)} %broadcast_in_dim.57), kind=kOutput, calls=%fused_computation.53.clone.1 | convolution fusion | flops 458292480 | bytes 7871488 | tf_op jit(solution)/shard_map/while/body/eval_jaxpr/dot_general | solution.py:29
  154.7 2.7 %fusion.54 = bf16[2304,768]{1,0:T(8,128)(2,1)S(1)} fusion(bf16[2304,768]{1,0:T(8,128)(2,1)S(1)} %get-tuple-element.275, s32[]{:T(128)S(6)} %select_n.35, f32[768,2304]{1,0:T(8,128)S(1)} %get-tuple-element.255, f32[768]{0:T(1024)S(1)} %log_add_fusion.2, bf16[768,768]{1,0:T(8,128)(2,1)} %get-tuple-element.290), kind=kOutput, calls=%fused_computation.9.clone.1 | convolution fusion | flops 456818688 | bytes 7869440 | tf_op jit(solution)/shard_map/while/body/eval_jaxpr/dot_general | solution.py:35
  157.4 2.7 %multiply_reduce_fusion.2 = (f32[768]{0:T(1024)S(1)}, f32[768,2304]{1,0:T(8,128)S(1)}) fusion(f32[768,2304]{1,0:T(8,128)S(1)} %get-tuple-element.255, f32[768]{0:T(1024)S(1)} %log_add_fusion.2, bf16[1,2304,768]{2,1,0:T(8,128)(2,1)S(1)} %get-tuple-element.257, s32[]{:T(128)S(6)} %select_n.35, bf16[768,768]{1,0:T(8,128)(2,1)} %get-tuple-element.290), kind=kOutput, calls=%fused_computation.2.clone.1 | convolution fusion | flops 458292480 | bytes 14950400 | tf_op jit(solution)/shard_map/while/body/eval_jaxpr/dot_general | solution.py:29
  160.1 2.0 multiply_convert_fusion.2
  163.8 3.0 %fusion.53 = bf16[2304,768]{1,0:T(8,128)(2,1)} fusion(bf16[2304,768]{1,0:T(8,128)(2,1)} %get-tuple-element.274, s32[]{:T(128)S(6)} %select_n.35, bf16[768,2304]{1,0:T(8,128)(2,1)S(1)} %multiply_convert_fusion.2, bf16[768,768]{1,0:T(8,128)(2,1)} %get-tuple-element.288), kind=kOutput, calls=%fused_computation.11.clone.1 | convolution fusion | flops 453574656 | bytes 4326400 | tf_op jit(solution)/shard_map/while/body/eval_jaxpr/dot_general | solution.py:35
  166.8 1.9 slice_bitcast_fusion.6
  169.0 4.4 %collective-permute-start.3 = (bf16[2,768,768]{2,1,0:T(8,128)(2,1)S(1)}, bf16[2,768,768]{2,1,0:T(8,128)(2,1)S(1)}, u32[]{:S(2)}, u32[]{:S(2)}) collective-permute-start(bf16[2,768,768]{2,1,0:T(8,128)(2,1)S(1)} %pad_maximum_fusion.3), channel_id=1, source_target_pairs={{0,1},{1,4},{4,5},{5,8},{8,9},{9,12},{12,13},{2,3},{3,6},{6,7},{7,... | collective-permute-start | bytes 7077896 | tf_op jit(solution)/shard_map/ppermute | solution.py:25
  175.5 23.6 %collective-permute-done.3 = bf16[2,768,768]{2,1,0:T(8,128)(2,1)S(1)} collective-permute-done((bf16[2,768,768]{2,1,0:T(8,128)(2,1)S(1)}, bf16[2,768,768]{2,1,0:T(8,128)(2,1)S(1)}, u32[]{:S(2)}, u32[]{:S(2)}) %collective-permute-start.3) | collective-permute-done | bytes 2359328 | tf_op jit(solution)/shard_map/ppermute | solution.py:25
  199.2 4.6 %collective-permute-done.2 = bf16[2,768,768]{2,1,0:T(8,128)(2,1)S(1)} collective-permute-done((bf16[2,768,768]{2,1,0:T(8,128)(2,1)S(1)}, bf16[2,768,768]{2,1,0:T(8,128)(2,1)S(1)}, u32[]{:S(2)}, u32[]{:S(2)}) %collective-permute-start.2) | collective-permute-done | bytes 2359328 | tf_op jit(solution)/shard_map/ppermute | solution.py:25
  203.8 3.6 %fusion.26 = (bf16[768,768]{1,0:T(8,128)(2,1)}, bf16[768,768]{1,0:T(8,128)(2,1)}) fusion(bf16[2,768,768]{2,1,0:T(8,128)(2,1)S(1)} %collective-permute-done.3, bf16[2,768,768]{2,1,0:T(8,128)(2,1)S(1)} %collective-permute-done.2, bf16[2304,768]{1,0:T(8,128)(2,1)S(1)} %get-tuple-element.146, bf16[2304,768]{1,0:T(8,128)(2,1)} %get-tuple-element.145), kind=kLoop, calls=%fused_computation.38 | loop fusion | flops 7077888 | bytes 9437184 | tf_op jit(solution)/shard_map/convert_element_type | solution.py:113
  (44 shorter events, 23.5 us)
Async XLA Ops:
  0.6 36.0 %copy-start = (bf16[768,768]{1,0:T(8,128)(2,1)S(1)}, bf16[768,768]{1,0:T(8,128)(2,1)}, u32[]{:S(2)}) copy-start(bf16[768,768]{1,0:T(8,128)(2,1)} %param.9) | copy-start | bytes 3538948
  0.6 36.0 %copy-start.1 = (bf16[768,768]{1,0:T(8,128)(2,1)S(1)}, bf16[768,768]{1,0:T(8,128)(2,1)}, u32[]{:S(2)}) copy-start(bf16[768,768]{1,0:T(8,128)(2,1)} %param.8) | copy-start | bytes 3538948
  0.7 10.0 %copy-start.2 = (s32[8]{0:T(128)S(1)}, s32[8]{0:T(128)}, u32[]{:S(2)}) copy-start(s32[8]{0:T(128)} %param.11) | copy-start | bytes 100
  4.1 31.4 %collective-permute-start.1 = (bf16[2,768,768]{2,1,0:T(8,128)(2,1)}, bf16[2,768,768]{2,1,0:T(8,128)(2,1)}, u32[]{:S(2)}, u32[]{:S(2)}) collective-permute-start(bf16[2,768,768]{2,1,0:T(8,128)(2,1)} %pad_maximum_fusion.1), channel_id=1, source_target_pairs={{1,0},{4,1},{5,4},{8,5},{9,8},{12,9},{13,12},{3,2},{6,3},{7,6},{10... | collective-permute-start | bytes 7077896 | tf_op jit(solution)/shard_map/ppermute | solution.py:17
  6.0 30.6 %collective-permute-start = (bf16[2,768,768]{2,1,0:T(8,128)(2,1)}, bf16[2,768,768]{2,1,0:T(8,128)(2,1)}, u32[]{:S(2)}, u32[]{:S(2)}) collective-permute-start(bf16[2,768,768]{2,1,0:T(8,128)(2,1)} %pad_maximum_fusion.1), channel_id=1, source_target_pairs={{0,1},{1,4},{4,5},{5,8},{8,9},{9,12},{12,13},{2,3},{3,6},{6,7},{7,... | collective-permute-start | bytes 7077896 | tf_op jit(solution)/shard_map/ppermute | solution.py:16
  169.0 30.2 %collective-permute-start.3 = (bf16[2,768,768]{2,1,0:T(8,128)(2,1)S(1)}, bf16[2,768,768]{2,1,0:T(8,128)(2,1)S(1)}, u32[]{:S(2)}, u32[]{:S(2)}) collective-permute-start(bf16[2,768,768]{2,1,0:T(8,128)(2,1)S(1)} %pad_maximum_fusion.3), channel_id=1, source_target_pairs={{0,1},{1,4},{4,5},{5,8},{8,9},{9,12},{12,13},{2,3},{3,6},{6,7},{7,... | collective-permute-start | bytes 7077896 | tf_op jit(solution)/shard_map/ppermute | solution.py:25
  173.6 30.2 %collective-permute-start.2 = (bf16[2,768,768]{2,1,0:T(8,128)(2,1)S(1)}, bf16[2,768,768]{2,1,0:T(8,128)(2,1)S(1)}, u32[]{:S(2)}, u32[]{:S(2)}) collective-permute-start(bf16[2,768,768]{2,1,0:T(8,128)(2,1)S(1)} %pad_maximum_fusion.2), channel_id=1, source_target_pairs={{1,0},{4,1},{5,4},{8,5},{9,8},{12,9},{13,12},{3,2},{6,3},{7,6},{10... | collective-permute-start | bytes 7077896 | tf_op jit(solution)/shard_map/ppermute | solution.py:25
where the time goes:
time: 208 us; the launch traced here: 207 us
  matrix products  73.9 us (36%)
  waiting for transfers between devices  51.1 us (25%)
  other arithmetic  38.5 us (19%)
  local copies, waits for them, and re-layouts  27.7 us (13%)
  starting transfers between devices  12.8 us (6%)
  between operations  3.29 us (2%)
    dot_general x12, matrix products, tn_product(): lax.dot_general(left, right, (((0,), (0,)), ((), ())), preferred_element_...  34.2 us
    dot_general x12, matrix products, nt_product(): lax.dot_general(left, right, (((1,), (1,)), ((), ())), preferred_element_...  29 us
    ppermute x2, waiting for transfers between devices, from_behind(): return lax.ppermute(value, axis, pairs)  28.2 us
    ppermute x1, waiting for transfers between devices, padded(): after = lax.ppermute(first, axis, down)  21.6 us
    slice x6, local copies, waits for them, and re-layouts, one_head(): k_head = lax.dynamic_slice_in_dim(neighbour_kv[0], head_start, HEAD_DIM, 1)  21.2 us
    concatenate x1, other arithmetic, padded(): value = jnp.concatenate([before, value, after], axis=dim)  12.4 us
    convert_element_type x6, other arithmetic, one_head(): dscores = (probs * (dprob - row_delta)).astype(jnp.bfloat16)  11.9 us
    dot_general x6, matrix products, nn_product(): return jnp.dot(left, right, preferred_element_type=jnp.float32)  10.6 us
  transfers between devices with their start and end apart: 4, of which 4 were waited for; matrix products, arithmetic and copies ran while one was open for 0% of the time, Pallas kernels for 0%

commit v1 on v0

v1 whole, which is shorter than its diff:
```python
import functools
import math

import jax
import jax.numpy as jnp
from jax import lax
from jax.experimental import pallas as pl
from jax.experimental.pallas import tpu as pltpu
from jax.sharding import PartitionSpec as P

HEAD_DIM = 128
QUERY_TILE = 256
SCALE = HEAD_DIM ** -0.5
SCALE_LOG2 = SCALE * math.log2(math.e)
MESH = pl.DeviceIdType.MESH


def nt_product(left, right):
    return lax.dot_general(
        left, right, (((1,), (1,)), ((), ())), preferred_element_type=jnp.float32
    )


def tn_product(left, right):
    return lax.dot_general(
        left, right, (((0,), (0,)), ((), ())), preferred_element_type=jnp.float32
    )


def nn_product(left, right):
    return jnp.dot(left, right, preferred_element_type=jnp.float32)


def attention_kernel(
    bias_ref, q_hbm, k_hbm, v_hbm, g_hbm, dq_hbm, dk_hbm, dv_hbm,
    q_all, g_all, k_all, v_all, sent, got, own, dq_all, acc,
    load_sem, kv_send, kv_recv, term_send, term_recv, out_sem,
):
    row_tok, width = q_all.shape
    heads = width // HEAD_DIM
    reps = lax.axis_size("rep")
    count = lax.axis_size("ctx") * reps
    position = lax.axis_index("ctx") * reps + lax.axis_index("rep")
    has_low, has_high = position > 0, position < count - 1

    def device(index):
        return {"ctx": index // reps, "rep": lax.rem(index, reps)}

    high = device(jnp.minimum(position + 1, count - 1))
    low = device(jnp.maximum(position - 1, 0))
    targets = (high, low)
    sends = (has_high, has_low)
    receives = (has_low, has_high)

    def strip(head):
        return pl.ds(pl.multiple_of(head * HEAD_DIM, HEAD_DIM), HEAD_DIM)

    def kv_copies(head, way):
        columns = strip(head)
        return [
            pltpu.make_async_remote_copy(
                src_ref=source.at[:, columns],
                dst_ref=target.at[2 * way, :, columns],
                send_sem=kv_send.at[way, head, which],
                recv_sem=kv_recv.at[way, head, which],
                device_id=targets[way],
                device_id_type=MESH,
            )
            for which, (source, target) in enumerate(((k_hbm, k_all), (v_hbm, v_all)))
        ]

    def term_copy(head, way):
        columns = strip(head)
        return pltpu.make_async_remote_copy(
            src_ref=sent.at[way, :, :, columns],
            dst_ref=got.at[way, :, :, columns],
            send_sem=term_send.at[way, head],
            recv_sem=term_recv.at[way, head],
            device_id=targets[way],
            device_id_type=MESH,
        )

    def out_copy(head, which):
        columns = strip(head)
        source = (dq_all, own.at[0], own.at[1])[which]
        target = (dq_hbm, dk_hbm, dv_hbm)[which]
        return pltpu.make_async_copy(
            source.at[:, columns], target.at[:, columns], out_sem.at[which, head]
        )

    def send_kv(head):
        for way in range(2):
            @pl.when(sends[way])
            def _():
                for copy in kv_copies(head, way):
                    copy.start()

    loads = [
        pltpu.make_async_copy(source, target, load_sem.at[index])
        for index, (source, target) in enumerate(
            ((q_hbm, q_all), (k_hbm, k_all.at[1]), (v_hbm, v_all.at[1]), (g_hbm, g_all))
        )
    ]
    barrier = pltpu.get_barrier_semaphore()
    for way in range(2):
        @pl.when(sends[way])
        def _():
            pl.semaphore_signal(barrier, inc=1, device_id=targets[way], device_id_type=MESH)
    for load in loads:
        load.start()
    pl.semaphore_wait(barrier, has_low.astype(jnp.int32) + has_high.astype(jnp.int32))
    for head in range(min(2, heads)):
        send_kv(head)
    for way in range(2):
        @pl.when(jnp.logical_not(receives[way]))
        def _():
            k_all[2 * way] = jnp.zeros((row_tok, width), jnp.bfloat16)
            v_all[2 * way] = jnp.zeros((row_tok, width), jnp.bfloat16)
            got[way] = jnp.zeros((2, row_tok, width), jnp.bfloat16)
    for load in loads:
        load.wait()

    biases = (bias_ref[0], bias_ref[1], bias_ref[2])

    def combine(head):
        columns = strip(head)
        for way in range(2):
            @pl.when(receives[way])
            def _():
                term_copy(head, way).wait_recv()
        for which in range(2):
            total = own[which, :, columns].astype(jnp.float32)
            for way in range(2):
                total = total + got[way, which, :, columns].astype(jnp.float32)
            own[which, :, columns] = total.astype(jnp.bfloat16)
            out_copy(head, 1 + which).start()

    def one_head(head, carry):
        columns = strip(head)
        for way in range(2):
            @pl.when(receives[way])
            def _():
                for copy in kv_copies(head, way):
                    copy.wait_recv()

        @pl.when(head + 2 < heads)
        def _():
            send_kv(head + 2)

        acc[...] = jnp.zeros_like(acc)

        def one_tile(tile, inner):
            rows = pl.ds(pl.multiple_of(tile * QUERY_TILE, QUERY_TILE), QUERY_TILE)
            q_tile = q_all[rows, columns]
            g_tile = g_all[rows, columns]
            scores = [nt_product(k_all[b, :, columns], q_tile) for b in range(3)]
            tops = [
                jnp.max(scores[b], axis=0, keepdims=True) + biases[b] for b in range(3)
            ]
            top = jnp.maximum(jnp.maximum(tops[0], tops[1]), tops[2])
            weights = [
                jnp.exp2(scores[b] * SCALE_LOG2 - (top - biases[b]) * SCALE_LOG2)
                for b in range(3)
            ]
            total = sum(jnp.sum(w, axis=0, keepdims=True) for w in weights)
            inverse = 1.0 / total
            dprobs = [nt_product(v_all[b, :, columns], g_tile) for b in range(3)]
            delta = inverse * sum(
                jnp.sum(w * d, axis=0, keepdims=True) for w, d in zip(weights, dprobs)
            )
            dq_tile = jnp.zeros((QUERY_TILE, HEAD_DIM), jnp.float32)
            for b in range(3):
                keys = pl.ds(b * row_tok, row_tok)
                probs = weights[b] * inverse
                dscores = (probs * (dprobs[b] - delta)).astype(jnp.bfloat16)
                acc[1, keys, :] += nn_product(probs.astype(jnp.bfloat16), g_tile)
                acc[0, keys, :] += nn_product(dscores, q_tile)
                dq_tile = dq_tile + tn_product(dscores, k_all[b, :, columns])
            dq_all[rows, columns] = (dq_tile * SCALE).astype(jnp.bfloat16)
            return inner

        lax.fori_loop(0, row_tok // QUERY_TILE, one_tile, 0)
        for which in range(2):
            factor = (SCALE, 1.0)[which]
            for b in range(3):
                block = acc[which, b * row_tok : (b + 1) * row_tok, :] * factor
                block = block.astype(jnp.bfloat16)
                if b == 1:
                    own[which, :, columns] = block
                else:
                    sent[1 - b // 2, which, :, columns] = block
        for way in range(2):
            @pl.when(sends[way])
            def _():
                term_copy(head, way).start()
        out_copy(head, 0).start()

        @pl.when(head >= 2)
        def _():
            combine(head - 2)

        return carry

    lax.fori_loop(0, heads, one_head, 0)
    for head in range(max(heads - 2, 0), heads):
        combine(head)

    def finish(head, carry):
        for way in range(2):
            @pl.when(sends[way])
            def _():
                for copy in kv_copies(head, way):
                    copy.wait_send()
                term_copy(head, way).wait_send()
        for which in range(3):
            out_copy(head, which).wait()
        return carry

    lax.fori_loop(0, heads, finish, 0)


def per_device(queries, keys_in, values, grad_out, clip_ids):
    row_tok, width = queries.shape
    heads = width // HEAD_DIM
    position = lax.axis_index(("ctx", "rep"))
    row_count = lax.axis_size(("ctx", "rep"))
    around = position + jnp.arange(-1, 2, dtype=jnp.int32)
    inside = (around >= 0) & (around < row_count)
    clips = clip_ids[jnp.clip(around, 0, row_count - 1)]
    bias = jnp.where(inside & (clips == clips[1]), 0.0, -jnp.inf).astype(jnp.float32)
    shape = jax.ShapeDtypeStruct((row_tok, width), jnp.bfloat16)
    anywhere = pl.BlockSpec(memory_space=pl.ANY)
    low = jnp.bfloat16
    return pl.pallas_call(
        attention_kernel,
        out_shape=(shape, shape, shape),
        in_specs=[pl.BlockSpec(memory_space=pltpu.SMEM)] + [anywhere] * 4,
        out_specs=(anywhere, anywhere, anywhere),
        scratch_shapes=[
            pltpu.VMEM((row_tok, width), low),
            pltpu.VMEM((row_tok, width), low),
            pltpu.VMEM((3, row_tok, width), low),
            pltpu.VMEM((3, row_tok, width), low),
            pltpu.VMEM((2, 2, row_tok, width), low),
            pltpu.VMEM((2, 2, row_tok, width), low),
            pltpu.VMEM((2, row_tok, width), low),
            pltpu.VMEM((row_tok, width), low),
            pltpu.VMEM((2, 3 * row_tok, HEAD_DIM), jnp.float32),
            pltpu.SemaphoreType.DMA((4,)),
            pltpu.SemaphoreType.DMA((2, heads, 2)),
            pltpu.SemaphoreType.DMA((2, heads, 2)),
            pltpu.SemaphoreType.DMA((2, heads)),
            pltpu.SemaphoreType.DMA((2, heads)),
            pltpu.SemaphoreType.DMA((3, heads)),
        ],
        compiler_params=pltpu.CompilerParams(
            collective_id=0, has_side_effects=True, vmem_limit_bytes=58 * 1024 * 1024
        ),
    )(bias, queries, keys_in, values, grad_out)


def solution(mesh):
    tokens = P(("groups", "ctx", "rep"), "head")
    return jax.shard_map(
        per_device,
        mesh=mesh,
        in_specs=(tokens, tokens, tokens, tokens, P("groups")),
        out_specs=(tokens, tokens, tokens),
        check_vma=False,
    )
```

time: 208 us -> 81.2 us (0.39)
  matrix products: 73.9 us -> 0 us
  Pallas kernels: 0 us -> 72.1 us
  waiting for transfers between devices: 51.1 us -> 0 us
  other arithmetic: 38.5 us -> 1.18 us
  local copies, waits for them, and re-layouts: 27.7 us -> 7.01 us
  starting transfers between devices: 12.8 us -> 0 us
  between operations: 3.29 us -> 0.68 us
    dot_general x30 -> x0, matrix products: 73.9 us -> none  [the longest x12 34.2 us: tn_product(): lax.dot_general(left, right, (((0,), (0,)), ((), ())), preferred_element_...]
    pallas_call x0 -> x1, Pallas kernels: none -> 72.1 us  [per_device(): pl.pallas_call(attention_kernel, out_shape=(shape, shape, shape), in_spec...]
    ppermute x4 -> x0, waiting for transfers between devices: 51.1 us -> none  [the longest x2 28.2 us: from_behind(): return lax.ppermute(value, axis, pairs)]
    slice x6 -> x1, local copies, waits for them, and re-layouts: 21.2 us -> 0.59 us  [per_device(): clips[1]]
    convert_element_type x7 -> x0, other arithmetic: 15.5 us -> none  [the longest x6 11.9 us: one_head(): dscores = (probs * (dprob - row_delta)).astype(jnp.bfloat16)]
    ppermute x4 -> x0, starting transfers between devices: 12.8 us -> none  [the longest x2 6.32 us: from_behind(): return lax.ppermute(value, axis, pairs)]
    concatenate x1 -> x0, other arithmetic: 12.4 us -> none  [padded(): value = jnp.concatenate([before, value, after], axis=dim)]
    reduce_sum x6 -> x0, other arithmetic: 6.64 us -> none  [one_head(): jnp.sum(jnp.exp(scores - row_max), axis=1, keepdims=True)]
  transfers between devices with their start and end apart: 4 -> 0, of which waited for: 4 -> 0; matrix products, arithmetic and copies ran while one was open for 0% -> 0% of each run, Pallas kernels for 0% -> 0%
where the time goes in v1:
time: 81.2 us; the launch traced here: 81 us
  Pallas kernels  72.1 us (89%)
  local copies, waits for them, and re-layouts  7.01 us (9%)
  other arithmetic  1.18 us (1%)
    pallas_call x1, Pallas kernels, per_device(): pl.pallas_call(attention_kernel, out_shape=(shape, shape, shape), in_spec...  72.1 us
    unnamed x9, local copies, waits for them, and re-layouts  5.79 us

profile of v1, /device:TPU:1, one launch (start us, length us, event | category | flops | bytes accessed | tf_op | source)
XLA Modules:
  0.0 81.0 jit_solution(17054006971897824372)
XLA Ops:
  0.6 0.0 copy-start
  0.7 0.6 copy-done
  1.3 0.6 gather_fusion
  1.9 0.6 slice.3
  2.5 1.2 %and_select_fusion.bias_ref = f32[3]{0:T(128)} fusion(s32[3]{0:T(128)S(1)} %gather_fusion, s32[]{:T(128)} %bitcast.1, s32[]{:T(128)S(6)} %add.42), kind=kLoop, calls=%fused_computation.3 | loop fusion | flops 24 | bytes 32 | tf_op jit(solution)/shard_map/jit(_where)/select_n | solution.py:230
  3.7 72.1 %shard_map.76 = (bf16[768,768]{1,0:T(8,128)(2,1)}, bf16[768,768]{1,0:T(8,128)(2,1)}, bf16[768,768]{1,0:T(8,128)(2,1)}) custom-call(f32[3]{0:T(128)} %and_select_fusion.bias_ref, bf16[768,768]{1,0:T(8,128)(2,1)} %q_hbm.1, bf16[768,768]{1,0:T(8,128)(2,1)} %k_hbm.1, bf16[768,768]{1,0:T(8,128)(2,1)} %v_hbm.1, bf16[768,768]{1,0:T(8,128)(2,1)} %g_hbm.1), custom_call_target="tpu_custom_call" | custom-call | tf_op jit(solution)/shard_map/pallas_call | solution.py:234
  75.8 0.0 copy-start.2
  75.8 2.5 %copy.11 = bf16[768,768]{1,0:T(8,128)(2,1)} copy(bf16[768,768]{1,0:T(8,128)(2,1)} %get-tuple-element.6) | data formatting | bytes 2359296
  78.2 0.0 copy-done.2
  78.2 0.0 copy-start.1
  78.2 1.0 %copy.12 = bf16[768,768]{1,0:T(8,128)(2,1)} copy(bf16[768,768]{1,0:T(8,128)(2,1)S(1)} %copy-done.2) | data formatting | bytes 2359296
  79.3 0.7 copy-done.1
  79.9 1.0 %copy.13 = bf16[768,768]{1,0:T(8,128)(2,1)} copy(bf16[768,768]{1,0:T(8,128)(2,1)S(1)} %copy-done.1) | data formatting | bytes 2359296
  (2 shorter events, 0.0 us)
Async XLA Ops:
  0.6 0.7 copy-start
  75.8 2.5 %copy-start.2 = (bf16[768,768]{1,0:T(8,128)(2,1)S(1)}, bf16[768,768]{1,0:T(8,128)(2,1)}, u32[]{:S(2)}) copy-start(bf16[768,768]{1,0:T(8,128)(2,1)} %get-tuple-element.7) | copy-start | bytes 3538948
  78.2 1.7 %copy-start.1 = (bf16[768,768]{1,0:T(8,128)(2,1)S(1)}, bf16[768,768]{1,0:T(8,128)(2,1)}, u32[]{:S(2)}) copy-start(bf16[768,768]{1,0:T(8,128)(2,1)} %get-tuple-element.8) | copy-start | bytes 3538948

commit v2 on v1

--- a/solution.py
+++ b/solution.py
@@ -9,7 +9,8 @@
 from jax.sharding import PartitionSpec as P
 
 HEAD_DIM = 128
-QUERY_TILE = 256
+KEY_CHUNK = 32
+LANES = 8
 SCALE = HEAD_DIM ** -0.5
 SCALE_LOG2 = SCALE * math.log2(math.e)
 MESH = pl.DeviceIdType.MESH
@@ -32,8 +33,9 @@
 
 
 def attention_kernel(
-    bias_ref, q_hbm, k_hbm, v_hbm, g_hbm, dq_hbm, dk_hbm, dv_hbm,
-    q_all, g_all, k_all, v_all, sent, got, own, dq_all, acc,
+    clip_ref, q_hbm, k_hbm, v_hbm, g_hbm, dq_hbm, dk_hbm, dv_hbm,
+    q_all, g_all, k_all, v_all, sent, got, own, dq_all,
+    weights, dprobs, probs_low, dscores,
     load_sem, kv_send, kv_recv, term_send, term_recv, out_sem,
 ):
     row_tok, width = q_all.shape
@@ -120,7 +122,14 @@
     for load in loads:
         load.wait()
 
-    biases = (bias_ref[0], bias_ref[1], bias_ref[2])
+    own_clip = clip_ref[position]
+    low_clip = clip_ref[jnp.maximum(position - 1, 0)]
+    high_clip = clip_ref[jnp.minimum(position + 1, count - 1)]
+    biases = (
+        jnp.where(has_low & (low_clip == own_clip), 0.0, -jnp.inf),
+        0.0,
+        jnp.where(has_high & (high_clip == own_clip), 0.0, -jnp.inf),
+    )
 
     def combine(head):
         columns = strip(head)
@@ -147,48 +156,52 @@
         def _():
             send_kv(head + 2)
 
-        acc[...] = jnp.zeros_like(acc)
-
-        def one_tile(tile, inner):
-            rows = pl.ds(pl.multiple_of(tile * QUERY_TILE, QUERY_TILE), QUERY_TILE)
-            q_tile = q_all[rows, columns]
-            g_tile = g_all[rows, columns]
-            scores = [nt_product(k_all[b, :, columns], q_tile) for b in range(3)]
-            tops = [
-                jnp.max(scores[b], axis=0, keepdims=True) + biases[b] for b in range(3)
-            ]
-            top = jnp.maximum(jnp.maximum(tops[0], tops[1]), tops[2])
-            weights = [
-                jnp.exp2(scores[b] * SCALE_LOG2 - (top - biases[b]) * SCALE_LOG2)
-                for b in range(3)
-            ]
-            total = sum(jnp.sum(w, axis=0, keepdims=True) for w in weights)
-            inverse = 1.0 / total
-            dprobs = [nt_product(v_all[b, :, columns], g_tile) for b in range(3)]
-            delta = inverse * sum(
-                jnp.sum(w * d, axis=0, keepdims=True) for w, d in zip(weights, dprobs)
-            )
-            dq_tile = jnp.zeros((QUERY_TILE, HEAD_DIM), jnp.float32)
-            for b in range(3):
-                keys = pl.ds(b * row_tok, row_tok)
-                probs = weights[b] * inverse
-                dscores = (probs * (dprobs[b] - delta)).astype(jnp.bfloat16)
-                acc[1, keys, :] += nn_product(probs.astype(jnp.bfloat16), g_tile)
-                acc[0, keys, :] += nn_product(dscores, q_tile)
-                dq_tile = dq_tile + tn_product(dscores, k_all[b, :, columns])
-            dq_all[rows, columns] = (dq_tile * SCALE).astype(jnp.bfloat16)
-            return inner
-
-        lax.fori_loop(0, row_tok // QUERY_TILE, one_tile, 0)
-        for which in range(2):
-            factor = (SCALE, 1.0)[which]
-            for b in range(3):
-                block = acc[which, b * row_tok : (b + 1) * row_tok, :] * factor
-                block = block.astype(jnp.bfloat16)
-                if b == 1:
-                    own[which, :, columns] = block
-                else:
-                    sent[1 - b // 2, which, :, columns] = block
+        q_head, g_head = q_all[:, columns], g_all[:, columns]
+        chunks = [pl.ds(start, KEY_CHUNK) for start in range(0, row_tok, KEY_CHUNK)]
+
+        def folded(value, op):
+            return op(value.reshape(KEY_CHUNK // LANES, LANES, row_tok), axis=0)
+
+        top = None
+        for b in range(3):
+            weights[b] = nt_product(k_all[b, :, columns], q_head)
+            block_top = None
+            for chunk in chunks:
+                part = folded(weights[b, chunk, :], jnp.max)
+                block_top = part if block_top is None else jnp.maximum(block_top, part)
+            block_top = jnp.max(block_top, axis=0, keepdims=True) + biases[b]
+            top = block_top if top is None else jnp.maximum(top, block_top)
+        total = jnp.zeros((LANES, row_tok), jnp.float32)
+        delta = jnp.zeros((LANES, row_tok), jnp.float32)
+        for b in range(3):
+            dprobs[b] = nt_product(v_all[b, :, columns], g_head)
+            shift = (top - biases[b]) * SCALE_LOG2
+            for chunk in chunks:
+                weight = jnp.exp2(weights[b, chunk, :] * SCALE_LOG2 - shift)
+                weights[b, chunk, :] = weight
+                total = total + folded(weight, jnp.sum)
+                delta = delta + folded(weight * dprobs[b, chunk, :], jnp.sum)
+        inverse = 1.0 / jnp.sum(total, axis=0, keepdims=True)
+        delta = inverse * jnp.sum(delta, axis=0, keepdims=True)
+        dq_head = None
+        for b in (0, 2, 1):
+            for chunk in chunks:
+                probs = weights[b, chunk, :] * inverse
+                probs_low[b, chunk, :] = probs.astype(jnp.bfloat16)
+                dscores[b, chunk, :] = (probs * (dprobs[b, chunk, :] - delta)).astype(
+                    jnp.bfloat16
+                )
+            value_term = nn_product(probs_low[b], g_head).astype(jnp.bfloat16)
+            key_term = (nn_product(dscores[b], q_head) * SCALE).astype(jnp.bfloat16)
+            part = tn_product(dscores[b], k_all[b, :, columns])
+            dq_head = part if dq_head is None else dq_head + part
+            if b == 1:
+                own[0, :, columns] = key_term
+                own[1, :, columns] = value_term
+            else:
+                sent[1 - b // 2, 0, :, columns] = key_term
+                sent[1 - b // 2, 1, :, columns] = value_term
+        dq_all[:, columns] = (dq_head * SCALE).astype(jnp.bfloat16)
         for way in range(2):
             @pl.when(sends[way])
             def _():
@@ -222,12 +235,6 @@
 def per_device(queries, keys_in, values, grad_out, clip_ids):
     row_tok, width = queries.shape
     heads = width // HEAD_DIM
-    position = lax.axis_index(("ctx", "rep"))
-    row_count = lax.axis_size(("ctx", "rep"))
-    around = position + jnp.arange(-1, 2, dtype=jnp.int32)
-    inside = (around >= 0) & (around < row_count)
-    clips = clip_ids[jnp.clip(around, 0, row_count - 1)]
-    bias = jnp.where(inside & (clips == clips[1]), 0.0, -jnp.inf).astype(jnp.float32)
     shape = jax.ShapeDtypeStruct((row_tok, width), jnp.bfloat16)
     anywhere = pl.BlockSpec(memory_space=pl.ANY)
     low = jnp.bfloat16
@@ -245,7 +252,10 @@
             pltpu.VMEM((2, 2, row_tok, width), low),
             pltpu.VMEM((2, row_tok, width), low),
             pltpu.VMEM((row_tok, width), low),
-            pltpu.VMEM((2, 3 * row_tok, HEAD_DIM), jnp.float32),
+            pltpu.VMEM((3, row_tok, row_tok), jnp.float32),
+            pltpu.VMEM((3, row_tok, row_tok), jnp.float32),
+            pltpu.VMEM((3, row_tok, row_tok), low),
+            pltpu.VMEM((3, row_tok, row_tok), low),
             pltpu.SemaphoreType.DMA((4,)),
             pltpu.SemaphoreType.DMA((2, heads, 2)),
             pltpu.SemaphoreType.DMA((2, heads, 2)),
@@ -256,7 +266,7 @@
         compiler_params=pltpu.CompilerParams(
             collective_id=0, has_side_effects=True, vmem_limit_bytes=58 * 1024 * 1024
         ),
-    )(bias, queries, keys_in, values, grad_out)
+    )(clip_ids, queries, keys_in, values, grad_out)
 
 
 def solution(mesh):

time: 81.2 us -> 65 us (0.80)
  Pallas kernels: 72.1 us -> 59 us
  local copies, waits for them, and re-layouts: 7.01 us -> 5.17 us
  other arithmetic: 1.18 us -> 0 us
    pallas_call x1, Pallas kernels: 72.1 us -> 59 us  [per_device(): pl.pallas_call(attention_kernel, out_shape=(shape, shape, shape), in_spec...]
    select_n x2 -> x0, other arithmetic: 1.17 us -> none  [the longest x1 1.16 us: per_device(): jnp.where(inside & (clips == clips[1]), 0.0, -jnp.inf).astype(jnp.float32)]
    unnamed x9 -> x7, local copies, waits for them, and re-layouts: 5.79 us -> 5.17 us
where the time goes in v2:
time: 65 us; the launch traced here: 64.8 us
  Pallas kernels  59 us (91%)
  local copies, waits for them, and re-layouts  5.17 us (8%)
  between operations  0.65 us (1%)
    pallas_call x1, Pallas kernels, per_device(): pl.pallas_call(attention_kernel, out_shape=(shape, shape, shape), in_spec...  59 us
    unnamed x7, local copies, waits for them, and re-layouts  5.17 us

profile of v2, /device:TPU:1, one launch (start us, length us, event | category | flops | bytes accessed | tf_op | source)
XLA Modules:
  0.0 64.8 jit_solution(11620447064664430454)
XLA Ops:
  0.6 59.0 %shard_map.76 = (bf16[768,768]{1,0:T(8,128)(2,1)}, bf16[768,768]{1,0:T(8,128)(2,1)}, bf16[768,768]{1,0:T(8,128)(2,1)}) custom-call(s32[8]{0:T(128)} %clip_ref.1, bf16[768,768]{1,0:T(8,128)(2,1)} %q_hbm.1, bf16[768,768]{1,0:T(8,128)(2,1)} %k_hbm.1, bf16[768,768]{1,0:T(8,128)(2,1)} %v_hbm.1, bf16[768,768]{1,0:T(8,128)(2,1)} %g_hbm.1), custom_call_target="tpu_custom_call" | custom-call | tf_op jit(solution)/shard_map/pallas_call | solution.py:241
  59.6 0.0 copy-start.1
  59.6 2.5 %copy.11 = bf16[768,768]{1,0:T(8,128)(2,1)} copy(bf16[768,768]{1,0:T(8,128)(2,1)} %get-tuple-element.6) | data formatting | bytes 2359296
  62.1 0.0 copy-done.1
  62.1 0.0 copy-start
  62.1 1.0 %copy.12 = bf16[768,768]{1,0:T(8,128)(2,1)} copy(bf16[768,768]{1,0:T(8,128)(2,1)S(1)} %copy-done.1) | data formatting | bytes 2359296
  63.1 0.7 %copy-done = bf16[768,768]{1,0:T(8,128)(2,1)S(1)} copy-done((bf16[768,768]{1,0:T(8,128)(2,1)S(1)}, bf16[768,768]{1,0:T(8,128)(2,1)}, u32[]{:S(2)}) %copy-start) | copy-done | bytes 1179672
  63.8 1.0 %copy.13 = bf16[768,768]{1,0:T(8,128)(2,1)} copy(bf16[768,768]{1,0:T(8,128)(2,1)S(1)} %copy-done) | data formatting | bytes 2359296
Async XLA Ops:
  59.6 2.5 %copy-start.1 = (bf16[768,768]{1,0:T(8,128)(2,1)S(1)}, bf16[768,768]{1,0:T(8,128)(2,1)}, u32[]{:S(2)}) copy-start(bf16[768,768]{1,0:T(8,128)(2,1)} %get-tuple-element.7) | copy-start | bytes 3538948
  62.1 1.7 %copy-start = (bf16[768,768]{1,0:T(8,128)(2,1)S(1)}, bf16[768,768]{1,0:T(8,128)(2,1)}, u32[]{:S(2)}) copy-start(bf16[768,768]{1,0:T(8,128)(2,1)} %get-tuple-element.8) | copy-start | bytes 3538948

commit v3 on v2

--- a/solution.py
+++ b/solution.py
@@ -38,8 +38,7 @@
     weights, dprobs, probs_low, dscores,
     load_sem, kv_send, kv_recv, term_send, term_recv, out_sem,
 ):
-    row_tok, width = q_all.shape
-    heads = width // HEAD_DIM
+    heads, row_tok, _ = q_all.shape
     reps = lax.axis_size("rep")
     count = lax.axis_size("ctx") * reps
     position = lax.axis_index("ctx") * reps + lax.axis_index("rep")
@@ -58,24 +57,22 @@
         return pl.ds(pl.multiple_of(head * HEAD_DIM, HEAD_DIM), HEAD_DIM)
 
     def kv_copies(head, way):
-        columns = strip(head)
         return [
             pltpu.make_async_remote_copy(
-                src_ref=source.at[:, columns],
-                dst_ref=target.at[2 * way, :, columns],
+                src_ref=target.at[1, head],
+                dst_ref=target.at[2 * way, head],
                 send_sem=kv_send.at[way, head, which],
                 recv_sem=kv_recv.at[way, head, which],
                 device_id=targets[way],
                 device_id_type=MESH,
             )
-            for which, (source, target) in enumerate(((k_hbm, k_all), (v_hbm, v_all)))
+            for which, target in enumerate((k_all, v_all))
         ]
 
     def term_copy(head, way):
-        columns = strip(head)
         return pltpu.make_async_remote_copy(
-            src_ref=sent.at[way, :, :, columns],
-            dst_ref=got.at[way, :, :, columns],
+            src_ref=sent.at[way, head],
+            dst_ref=got.at[way, head],
             send_sem=term_send.at[way, head],
             recv_sem=term_recv.at[way, head],
             device_id=targets[way],
@@ -84,10 +81,10 @@
 
     def out_copy(head, which):
         columns = strip(head)
-        source = (dq_all, own.at[0], own.at[1])[which]
+        source = (dq_all.at[head], own.at[0, head], own.at[1, head])[which]
         target = (dq_hbm, dk_hbm, dv_hbm)[which]
         return pltpu.make_async_copy(
-            source.at[:, columns], target.at[:, columns], out_sem.at[which, head]
+            source, target.at[:, columns], out_sem.at[which, head]
         )
 
     def send_kv(head):
@@ -97,30 +94,43 @@
                 for copy in kv_copies(head, way):
                     copy.start()
 
-    loads = [
-        pltpu.make_async_copy(source, target, load_sem.at[index])
-        for index, (source, target) in enumerate(
-            ((q_hbm, q_all), (k_hbm, k_all.at[1]), (v_hbm, v_all.at[1]), (g_hbm, g_all))
-        )
-    ]
+    def loads(head):
+        columns = strip(head)
+        return [
+            pltpu.make_async_copy(source.at[:, columns], target, load_sem.at[index, head])
+            for index, (source, target) in enumerate(
+                (
+                    (k_hbm, k_all.at[1, head]),
+                    (v_hbm, v_all.at[1, head]),
+                    (q_hbm, q_all.at[head]),
+                    (g_hbm, g_all.at[head]),
+                )
+            )
+        ]
+
     barrier = pltpu.get_barrier_semaphore()
     for way in range(2):
         @pl.when(sends[way])
         def _():
             pl.semaphore_signal(barrier, inc=1, device_id=targets[way], device_id_type=MESH)
-    for load in loads:
-        load.start()
+    for head in range(heads):
+        for load in loads(head):
+            load.start()
     pl.semaphore_wait(barrier, has_low.astype(jnp.int32) + has_high.astype(jnp.int32))
-    for head in range(min(2, heads)):
-        send_kv(head)
+    for head in range(heads):
+        for load in loads(head)[:2]:
+            load.wait()
+        if head < 2:
+            send_kv(head)
     for way in range(2):
         @pl.when(jnp.logical_not(receives[way]))
         def _():
-            k_all[2 * way] = jnp.zeros((row_tok, width), jnp.bfloat16)
-            v_all[2 * way] = jnp.zeros((row_tok, width), jnp.bfloat16)
-            got[way] = jnp.zeros((2, row_tok, width), jnp.bfloat16)
-    for load in loads:
-        load.wait()
+            k_all[2 * way] = jnp.zeros((heads, row_tok, HEAD_DIM), jnp.bfloat16)
+            v_all[2 * way] = jnp.zeros((heads, row_tok, HEAD_DIM), jnp.bfloat16)
+            got[way] = jnp.zeros((heads, 2, row_tok, HEAD_DIM), jnp.bfloat16)
+    for head in range(heads):
+        for load in loads(head)[2:]:
+            load.wait()
 
     own_clip = clip_ref[position]
     low_clip = clip_ref[jnp.maximum(position - 1, 0)]
@@ -132,20 +142,18 @@
     )
 
     def combine(head):
-        columns = strip(head)
         for way in range(2):
             @pl.when(receives[way])
             def _():
                 term_copy(head, way).wait_recv()
         for which in range(2):
-            total = own[which, :, columns].astype(jnp.float32)
+            total = own[which, head].astype(jnp.float32)
             for way in range(2):
-                total = total + got[way, which, :, columns].astype(jnp.float32)
-            own[which, :, columns] = total.astype(jnp.bfloat16)
+                total = total + got[way, head, which].astype(jnp.float32)
+            own[which, head] = total.astype(jnp.bfloat16)
             out_copy(head, 1 + which).start()
 
     def one_head(head, carry):
-        columns = strip(head)
         for way in range(2):
             @pl.when(receives[way])
             def _():
@@ -156,7 +164,7 @@
         def _():
             send_kv(head + 2)
 
-        q_head, g_head = q_all[:, columns], g_all[:, columns]
+        q_head, g_head = q_all[head], g_all[head]
         chunks = [pl.ds(start, KEY_CHUNK) for start in range(0, row_tok, KEY_CHUNK)]
 
         def folded(value, op):
@@ -164,7 +172,7 @@
 
         top = None
         for b in range(3):
-            weights[b] = nt_product(k_all[b, :, columns], q_head)
+            weights[b] = nt_product(k_all[b, head], q_head)
             block_top = None
             for chunk in chunks:
                 part = folded(weights[b, chunk, :], jnp.max)
@@ -174,7 +182,7 @@
         total = jnp.zeros((LANES, row_tok), jnp.float32)
         delta = jnp.zeros((LANES, row_tok), jnp.float32)
         for b in range(3):
-            dprobs[b] = nt_product(v_all[b, :, columns], g_head)
+            dprobs[b] = nt_product(v_all[b, head], g_head)
             shift = (top - biases[b]) * SCALE_LOG2
             for chunk in chunks:
                 weight = jnp.exp2(weights[b, chunk, :] * SCALE_LOG2 - shift)
@@ -193,15 +201,15 @@
                 )
             value_term = nn_product(probs_low[b], g_head).astype(jnp.bfloat16)
             key_term = (nn_product(dscores[b], q_head) * SCALE).astype(jnp.bfloat16)
-            part = tn_product(dscores[b], k_all[b, :, columns])
+            part = tn_product(dscores[b], k_all[b, head])
             dq_head = part if dq_head is None else dq_head + part
             if b == 1:
-                own[0, :, columns] = key_term
-                own[1, :, columns] = value_term
+                own[0, head] = key_term
+                own[1, head] = value_term
             else:
-                sent[1 - b // 2, 0, :, columns] = key_term
-                sent[1 - b // 2, 1, :, columns] = value_term
-        dq_all[:, columns] = (dq_head * SCALE).astype(jnp.bfloat16)
+                sent[1 - b // 2, head, 0] = key_term
+                sent[1 - b // 2, head, 1] = value_term
+        dq_all[head] = (dq_head * SCALE).astype(jnp.bfloat16)
         for way in range(2):
             @pl.when(sends[way])
             def _():
@@ -232,31 +240,36 @@
     lax.fori_loop(0, heads, finish, 0)
 
 
+def place_kernel(*refs):
+    for source, target in zip(refs[:3], refs[3:]):
+        target[...] = source[...]
+
+
 def per_device(queries, keys_in, values, grad_out, clip_ids):
     row_tok, width = queries.shape
     heads = width // HEAD_DIM
     shape = jax.ShapeDtypeStruct((row_tok, width), jnp.bfloat16)
     anywhere = pl.BlockSpec(memory_space=pl.ANY)
     low = jnp.bfloat16
-    return pl.pallas_call(
+    grads = pl.pallas_call(
         attention_kernel,
         out_shape=(shape, shape, shape),
         in_specs=[pl.BlockSpec(memory_space=pltpu.SMEM)] + [anywhere] * 4,
         out_specs=(anywhere, anywhere, anywhere),
         scratch_shapes=[
-            pltpu.VMEM((row_tok, width), low),
-            pltpu.VMEM((row_tok, width), low),
-            pltpu.VMEM((3, row_tok, width), low),
-            pltpu.VMEM((3, row_tok, width), low),
-            pltpu.VMEM((2, 2, row_tok, width), low),
-            pltpu.VMEM((2, 2, row_tok, width), low),
-            pltpu.VMEM((2, row_tok, width), low),
-            pltpu.VMEM((row_tok, width), low),
+            pltpu.VMEM((heads, row_tok, HEAD_DIM), low),
+            pltpu.VMEM((heads, row_tok, HEAD_DIM), low),
+            pltpu.VMEM((3, heads, row_tok, HEAD_DIM), low),
+            pltpu.VMEM((3, heads, row_tok, HEAD_DIM), low),
+            pltpu.VMEM((2, heads, 2, row_tok, HEAD_DIM), low),
+            pltpu.VMEM((2, heads, 2, row_tok, HEAD_DIM), low),
+            pltpu.VMEM((2, heads, row_tok, HEAD_DIM), low),
+            pltpu.VMEM((heads, row_tok, HEAD_DIM), low),
             pltpu.VMEM((3, row_tok, row_tok), jnp.float32),
             pltpu.VMEM((3, row_tok, row_tok), jnp.float32),
             pltpu.VMEM((3, row_tok, row_tok), low),
             pltpu.VMEM((3, row_tok, row_tok), low),
-            pltpu.SemaphoreType.DMA((4,)),
+            pltpu.SemaphoreType.DMA((4, heads)),
             pltpu.SemaphoreType.DMA((2, heads, 2)),
             pltpu.SemaphoreType.DMA((2, heads, 2)),
             pltpu.SemaphoreType.DMA((2, heads)),
@@ -267,6 +280,14 @@
             collective_id=0, has_side_effects=True, vmem_limit_bytes=58 * 1024 * 1024
         ),
     )(clip_ids, queries, keys_in, values, grad_out)
+    block = pl.BlockSpec((row_tok // 3, width), lambda step: (step, 0))
+    return pl.pallas_call(
+        place_kernel,
+        grid=(3,),
+        out_shape=(shape, shape, shape),
+        in_specs=[block] * 3,
+        out_specs=(block, block, block),
+    )(*grads)
 
 
 def solution(mesh):

time: 65 us -> 64 us (0.985)
  local copies, waits for them, and re-layouts: 5.17 us -> 0 us
  Pallas kernels: 59 us -> 63.2 us
    unnamed x7 -> x0, local copies, waits for them, and re-layouts: 5.17 us -> none
    pallas_call x0 -> x1, Pallas kernels: none -> 4.57 us  [per_device(): pl.pallas_call(place_kernel, grid=(3,), out_shape=(shape, shape, shape),...]
where the time goes in v3:
time: 64 us; the launch traced here: 63.8 us
  Pallas kernels  63.2 us (99%)
  between operations  0.64 us (1%)
    pallas_call x1, Pallas kernels, per_device(): pl.pallas_call(attention_kernel, out_shape=(shape, shape, shape), in_spec...  58.6 us
    pallas_call x1, Pallas kernels, per_device(): pl.pallas_call(place_kernel, grid=(3,), out_shape=(shape, shape, shape),...  4.57 us

profile of v3, /device:TPU:1, one launch (start us, length us, event | category | flops | bytes accessed | tf_op | source)
XLA Modules:
  0.0 63.8 jit_solution(17184070554734472255)
XLA Ops:
  0.6 58.6 %shard_map.76 = (bf16[768,768]{1,0:T(8,128)(2,1)}, bf16[768,768]{1,0:T(8,128)(2,1)}, bf16[768,768]{1,0:T(8,128)(2,1)}) custom-call(s32[8]{0:T(128)} %clip_ref.1, bf16[768,768]{1,0:T(8,128)(2,1)} %q_hbm.1, bf16[768,768]{1,0:T(8,128)(2,1)} %k_hbm.1, bf16[768,768]{1,0:T(8,128)(2,1)} %v_hbm.1, bf16[768,768]{1,0:T(8,128)(2,1)} %g_hbm.1), custom_call_target="tpu_custom_call" | custom-call | tf_op jit(solution)/shard_map/pallas_call | solution.py:254
  59.2 4.6 %shard_map.77 = (bf16[768,768]{1,0:T(8,128)(2,1)}, bf16[768,768]{1,0:T(8,128)(2,1)}, bf16[768,768]{1,0:T(8,128)(2,1)}) custom-call(bf16[768,768]{1,0:T(8,128)(2,1)} %get-tuple-element.6.refs_0_, bf16[768,768]{1,0:T(8,128)(2,1)} %get-tuple-element.7.refs_1_, bf16[768,768]{1,0:T(8,128)(2,1)} %get-tuple-element.8.refs_2_), custom_call_target="tpu_custom_call" | custom-call | tf_op jit(solution)/shard_map/pallas_call | solution.py:284

commit v4 on v3

--- a/solution.py
+++ b/solution.py
@@ -280,10 +280,10 @@
             collective_id=0, has_side_effects=True, vmem_limit_bytes=58 * 1024 * 1024
         ),
     )(clip_ids, queries, keys_in, values, grad_out)
-    block = pl.BlockSpec((row_tok // 3, width), lambda step: (step, 0))
+    block = pl.BlockSpec((row_tok // 6, width), lambda step: (step, 0))
     return pl.pallas_call(
         place_kernel,
-        grid=(3,),
+        grid=(6,),
         out_shape=(shape, shape, shape),
         in_specs=[block] * 3,
         out_specs=(block, block, block),

time: 64 us -> 65 us (1.016)
  Pallas kernels: 63.2 us -> 64.1 us
    pallas_call x1, Pallas kernels: 4.57 us -> 5.47 us  [per_device(): pl.pallas_call(place_kernel, grid=(6,), out_shape=(shape, shape, shape),...]
where the time goes in v4:
time: 65 us; the launch traced here: 64.7 us
  Pallas kernels  64.1 us (99%)
    pallas_call x1, Pallas kernels, per_device(): pl.pallas_call(attention_kernel, out_shape=(shape, shape, shape), in_spec...  58.6 us
    pallas_call x1, Pallas kernels, per_device(): pl.pallas_call(place_kernel, grid=(6,), out_shape=(shape, shape, shape),...  5.47 us

profile of v4, /device:TPU:1, one launch (start us, length us, event | category | flops | bytes accessed | tf_op | source)
XLA Modules:
  0.0 64.7 jit_solution(17111329639089946841)
XLA Ops:
  0.6 58.6 %shard_map.76 = (bf16[768,768]{1,0:T(8,128)(2,1)}, bf16[768,768]{1,0:T(8,128)(2,1)}, bf16[768,768]{1,0:T(8,128)(2,1)}) custom-call(s32[8]{0:T(128)} %clip_ref.1, bf16[768,768]{1,0:T(8,128)(2,1)} %q_hbm.1, bf16[768,768]{1,0:T(8,128)(2,1)} %k_hbm.1, bf16[768,768]{1,0:T(8,128)(2,1)} %v_hbm.1, bf16[768,768]{1,0:T(8,128)(2,1)} %g_hbm.1), custom_call_target="tpu_custom_call" | custom-call | tf_op jit(solution)/shard_map/pallas_call | solution.py:254
  59.2 5.5 %shard_map.77 = (bf16[768,768]{1,0:T(8,128)(2,1)}, bf16[768,768]{1,0:T(8,128)(2,1)}, bf16[768,768]{1,0:T(8,128)(2,1)}) custom-call(bf16[768,768]{1,0:T(8,128)(2,1)} %get-tuple-element.6.refs_0_, bf16[768,768]{1,0:T(8,128)(2,1)} %get-tuple-element.7.refs_1_, bf16[768,768]{1,0:T(8,128)(2,1)} %get-tuple-element.8.refs_2_), custom_call_target="tpu_custom_call" | custom-call | tf_op jit(solution)/shard_map/pallas_call | solution.py:284
